TPU v7x, 512 devices: a whole 4x4x16 slice. The times are simulated.
512 devices in a mesh: pipe: 16 (over y, z_lo), dp: 32 (over z_hi, x, core).
Axes of the slice: x: 4, y: 4, z: 16 (z_hi: 4, z_lo: 4; z = z_hi * 4 + z_lo), core: 2. Of those that a mesh axis runs over, the one named last changes fastest.
Arguments:
- grad_out: bfloat16 [16, 2, 2, 128, 3584], P('pipe', None, None, 'dp'), may hold values from -6 to 6
- hidden: bfloat16 [16, 2, 2, 128, 9216], P('pipe', None, None, None, 'dp'), may hold values from -5 to 5
- weights: bfloat16 [16, 9216, 3584], P('pipe', 'dp'), may hold values from -5 to 5
- counts: int32 [16, 2, 2, 32], P('pipe', None, None, 'dp'), may hold values from 1 to 4
Outputs:
- grad_hidden: bfloat16 [16, 2, 2, 128, 9216], P('pipe', None, None, None, 'dp')
- new_weights: bfloat16 [16, 9216, 3584], P('pipe', 'dp')
All inputs are finite; a program needn't handle non-finite values.
Results may differ from a plain program's by a relative error of at most 0.0034.
Values may be sent and summed in bfloat16 or wider, within the bound.
No kernel may reach another device: no remote copies, remote signals or barrier semaphores. Data moves between devices by JAX's collectives and lax.ppermute only.
A program may use at most 64 MiB of HBM per device.

v0:
```python
import jax
import jax.numpy as jnp
from jax import lax
from jax.sharding import PartitionSpec as P

step_rate = 2.0


def from_partner(block, axis, apart):
    count = lax.axis_size(axis)
    route = []
    for low in range(count):
        high = low | 1 << apart
        if high != low and high < count:
            route += [(low, high), (high, low)]
    return lax.ppermute(block, axis, route)


def shards(grad_out, hidden, weights, counts):
    row_total = grad_out.shape[3]
    full_width = grad_out.shape[4]
    micro = hidden.shape[2]
    group_rows = hidden.shape[3]
    share = hidden.shape[4]
    scale_factor = float(full_width) ** (-0.5)
    slot_index = lax.broadcasted_iota(jnp.int32, (1, 1, 1, row_total), 3)
    live_rows = slot_index < counts
    masked = jnp.where(live_rows[..., None], grad_out, jnp.zeros_like(grad_out))
    own_weight = weights[0]
    pipe_bits = lax.axis_size("pipe").bit_length() - 1
    outgoing = jnp.concatenate(
        [masked[0, 1].reshape(micro, -1), hidden[0, 1].reshape(micro, -1)], axis=1
    )
    incoming = outgoing
    for fetch_bit_index in range(pipe_bits):
        incoming = from_partner(incoming, "pipe", fetch_bit_index)
    split_at = row_total * full_width
    mirror_masked = incoming[:, :split_at].reshape(micro, row_total, full_width)
    mirror_hidden = incoming[:, split_at:].reshape(micro, group_rows, share)
    mirror_masked, mirror_hidden = (mirror_masked, mirror_hidden)
    both_masked = jnp.stack([masked[0, 0], mirror_masked], axis=0)
    both_hidden = jnp.stack([hidden[0, 0], mirror_hidden], axis=0)
    piece = lax.all_gather(both_masked, "dp", axis=2, tiled=True)
    rows_out = jnp.einsum("rmkd,hd->rmkh", piece, own_weight, preferred_element_type=jnp.float32)
    grad_acc = rows_out
    weight_acc = jnp.einsum(
        "rmkh,rmkd->rhd", both_hidden, piece, preferred_element_type=jnp.float32
    )
    grad_acc, weight_acc = (grad_acc, weight_acc)
    grad_rows = (grad_acc * scale_factor).astype(jnp.bfloat16)
    partial_value = (weight_acc * scale_factor).astype(jnp.bfloat16)
    gradient = partial_value[0].astype(jnp.float32) + partial_value[1].astype(jnp.float32)
    new_weight = (own_weight.astype(jnp.float32) - step_rate * gradient).astype(jnp.bfloat16)
    returned = grad_rows[1]
    for bit_index in range(pipe_bits):
        returned = from_partner(returned, "pipe", bit_index)
    grad_hidden = jnp.stack([grad_rows[0], returned], axis=0)[None]
    return (grad_hidden, new_weight[None])


def solution(mesh):
    return jax.shard_map(
        shards,
        mesh=mesh,
        in_specs=(
            P("pipe", None, None, "dp", None),
            P("pipe", None, None, None, "dp"),
            P("pipe", "dp", None),
            P("pipe", None, None, "dp"),
        ),
        out_specs=(P("pipe", None, None, None, "dp"), P("pipe", "dp", None)),
        check_vma=False,
    )
```

profile of v0, /device:TPU:4, one launch (start us, length us, event | category | flops | bytes accessed | tf_op | source)
XLA Modules:
  0.0 193.9 jit_solution(3951308479756435278)
XLA Ops:
  7.2 0.0 all-gather.2.cloned.1.call-start
  7.2 0.7 iota_compare_fusion
  7.9 1.1 broadcast_select_fusion
  9.0 0.1 slice_bitcast_fusion.2
  9.0 1.0 slice_bitcast_fusion.1
  10.1 0.2 copy.9
  10.2 0.3 reshape_squeeze.7
  10.5 0.2 pad_maximum_fusion
  10.7 3.8 %collective-permute-start = (bf16[2,51200]{1,0:T(2,128)(2,1)S(1)}, bf16[2,51200]{1,0:T(2,128)(2,1)S(1)}, u32[]{:S(2)}, u32[]{:S(2)}) collective-permute-start(bf16[2,51200]{1,0:T(2,128)(2,1)S(1)} %pad_maximum_fusion), channel_id=1, source_target_pairs={{0,32},{32,0},{64,96},{96,64},{128,160},{160,128},{192,224},{224,1... | collective-permute-start | bytes 614408 | tf_op jit(solution)/shard_map/ppermute | solution.py:16
  14.6 5.1 %collective-permute-done = bf16[2,51200]{1,0:T(2,128)(2,1)S(1)} collective-permute-done((bf16[2,51200]{1,0:T(2,128)(2,1)S(1)}, bf16[2,51200]{1,0:T(2,128)(2,1)S(1)}, u32[]{:S(2)}, u32[]{:S(2)}) %collective-permute-start) | collective-permute-done | bytes 204832 | tf_op jit(solution)/shard_map/ppermute | solution.py:16
  19.6 5.2 %collective-permute-start.1 = (bf16[2,51200]{1,0:T(2,128)(2,1)S(1)}, bf16[2,51200]{1,0:T(2,128)(2,1)S(1)}, u32[]{:S(2)}, u32[]{:S(2)}) collective-permute-start(bf16[2,51200]{1,0:T(2,128)(2,1)S(1)} %collective-permute-done), channel_id=1, source_target_pairs={{0,64},{64,0},{32,96},{96,32},{128,192},{192,128},{160,224},{224,1... | collective-permute-start | bytes 614408 | tf_op jit(solution)/shard_map/ppermute | solution.py:16
  24.8 8.8 %collective-permute-done.1 = bf16[2,51200]{1,0:T(2,128)(2,1)S(1)} collective-permute-done((bf16[2,51200]{1,0:T(2,128)(2,1)S(1)}, bf16[2,51200]{1,0:T(2,128)(2,1)S(1)}, u32[]{:S(2)}, u32[]{:S(2)}) %collective-permute-start.1) | collective-permute-done | bytes 204832 | tf_op jit(solution)/shard_map/ppermute | solution.py:16
  33.6 3.5 %collective-permute-start.2 = (bf16[2,51200]{1,0:T(2,128)(2,1)S(1)}, bf16[2,51200]{1,0:T(2,128)(2,1)S(1)}, u32[]{:S(2)}, u32[]{:S(2)}) collective-permute-start(bf16[2,51200]{1,0:T(2,128)(2,1)S(1)} %collective-permute-done.1), channel_id=1, source_target_pairs={{0,128},{128,0},{32,160},{160,32},{64,192},{192,64},{96,224},{224,... | collective-permute-start | bytes 614408 | tf_op jit(solution)/shard_map/ppermute | solution.py:16
  37.1 4.4 %collective-permute-done.2 = bf16[2,51200]{1,0:T(2,128)(2,1)S(1)} collective-permute-done((bf16[2,51200]{1,0:T(2,128)(2,1)S(1)}, bf16[2,51200]{1,0:T(2,128)(2,1)S(1)}, u32[]{:S(2)}, u32[]{:S(2)}) %collective-permute-start.2) | collective-permute-done | bytes 204832 | tf_op jit(solution)/shard_map/ppermute | solution.py:16
  41.4 5.1 %collective-permute-start.3 = (bf16[2,51200]{1,0:T(2,128)(2,1)S(1)}, bf16[2,51200]{1,0:T(2,128)(2,1)S(1)}, u32[]{:S(2)}, u32[]{:S(2)}) collective-permute-start(bf16[2,51200]{1,0:T(2,128)(2,1)S(1)} %collective-permute-done.2), channel_id=1, source_target_pairs={{0,256},{256,0},{32,288},{288,32},{64,320},{320,64},{96,352},{352,... | collective-permute-start | bytes 614408 | tf_op jit(solution)/shard_map/ppermute | solution.py:16
  46.5 4.0 %collective-permute-done.3 = bf16[2,51200]{1,0:T(2,128)(2,1)S(1)} collective-permute-done((bf16[2,51200]{1,0:T(2,128)(2,1)S(1)}, bf16[2,51200]{1,0:T(2,128)(2,1)S(1)}, u32[]{:S(2)}, u32[]{:S(2)}) %collective-permute-start.3) | collective-permute-done | bytes 204832 | tf_op jit(solution)/shard_map/ppermute | solution.py:16
  50.6 0.8 pad_maximum_fusion.1
  51.5 93.9 %all-gather.2.cloned.1.call-done = bf16[2,2,128,3584]{3,1,0,2:T(2,128)(2,1)} async-done(((bf16[2,2,4,3584]{3,1,0,2:T(2,128)(2,1)}), bf16[2,2,128,3584]{3,1,0,2:T(2,128)(2,1)}) %all-gather.2.cloned.1.call-update) | async-done | bytes 3670032 | tf_op jit(solution)/shard_map/all_gather | solution.py:43
  145.4 4.0 %fusion.10 = bf16[2,2,128,288]{2,3,1,0:T(8,128)(2,1)S(1)} fusion(bf16[1,288,3584]{2,1,0:T(8,128)(2,1)} %param.6, bf16[2,2,128,3584]{3,1,0,2:T(2,128)(2,1)} %all-gather.2.cloned.1.call-done), kind=kOutput, calls=%fused_computation.8 | convolution fusion | flops 1057259520 | bytes 6029312 | tf_op jit(solution)/shard_map/rmkd,hd->rmkh/dot_general | solution.py:44
  149.4 1.9 collective-permute-start.4
  151.3 6.0 %collective-permute-done.4 = bf16[2,128,288]{1,2,0:T(8,128)(2,1)S(1)} collective-permute-done((bf16[2,128,288]{1,2,0:T(8,128)(2,1)S(1)}, bf16[2,128,288]{1,2,0:T(8,128)(2,1)S(1)}, u32[]{:S(2)}, u32[]{:S(2)}) %collective-permute-start.4) | collective-permute-done | bytes 147488 | tf_op jit(solution)/shard_map/ppermute | solution.py:16
  157.3 3.5 %collective-permute-start.5 = (bf16[2,128,288]{1,2,0:T(8,128)(2,1)S(1)}, bf16[2,128,288]{1,2,0:T(8,128)(2,1)S(1)}, u32[]{:S(2)}, u32[]{:S(2)}) collective-permute-start(bf16[2,128,288]{1,2,0:T(8,128)(2,1)S(1)} %collective-permute-done.4), channel_id=1, source_target_pairs={{0,64},{64,0},{32,96},{96,32},{128,192},{192,128},{160,224},{224,1... | collective-permute-start | bytes 442376 | tf_op jit(solution)/shard_map/ppermute | solution.py:16
  160.8 0.1 slice.45
  160.9 0.3 stack_reshape.7
  161.2 0.2 copy.12
  161.4 7.1 %collective-permute-done.5 = bf16[2,128,288]{1,2,0:T(8,128)(2,1)S(1)} collective-permute-done((bf16[2,128,288]{1,2,0:T(8,128)(2,1)S(1)}, bf16[2,128,288]{1,2,0:T(8,128)(2,1)S(1)}, u32[]{:S(2)}, u32[]{:S(2)}) %collective-permute-start.5) | collective-permute-done | bytes 147488 | tf_op jit(solution)/shard_map/ppermute | solution.py:16
  168.5 4.9 %collective-permute-start.6 = (bf16[2,128,288]{1,2,0:T(8,128)(2,1)S(1)}, bf16[2,128,288]{1,2,0:T(8,128)(2,1)S(1)}, u32[]{:S(2)}, u32[]{:S(2)}) collective-permute-start(bf16[2,128,288]{1,2,0:T(8,128)(2,1)S(1)} %collective-permute-done.5), channel_id=1, source_target_pairs={{0,128},{128,0},{32,160},{160,32},{64,192},{192,64},{96,224},{224,... | collective-permute-start | bytes 442376 | tf_op jit(solution)/shard_map/ppermute | solution.py:16
  173.4 4.1 %fusion = bf16[2,288,3584]{2,1,0:T(8,128)(2,1)S(1)} fusion(bf16[2,2,128,3584]{3,1,0,2:T(2,128)(2,1)} %all-gather.2.cloned.1.call-done, bf16[1,2,128,288]{2,3,1,0:T(8,128)(2,1)S(1)} %copy.12, bf16[1,2,128,288]{2,3,1,0:T(8,128)(2,1)S(1)} %get-tuple-element.2), kind=kOutput, calls=%fused_computation.1 | convolution fusion | flops 1061240832 | bytes 8093696 | tf_op jit(solution)/shard_map/rmkh,rmkd->rhd/dot_general | solution.py:46
  177.5 4.6 %collective-permute-start.7 = (bf16[2,128,288]{1,2,0:T(8,128)(2,1)S(1)}, bf16[2,128,288]{1,2,0:T(8,128)(2,1)S(1)}, u32[]{:S(2)}, u32[]{:S(2)}) collective-permute-start(bf16[2,128,288]{1,2,0:T(8,128)(2,1)S(1)} %collective-permute-done.6), channel_id=1, source_target_pairs={{0,256},{256,0},{32,288},{288,32},{64,320},{320,64},{96,352},{352,... | collective-permute-start | bytes 442376 | tf_op jit(solution)/shard_map/ppermute | solution.py:16
  182.1 2.2 %subtract_convert_fusion = bf16[1,288,3584]{2,1,0:T(8,128)(2,1)} fusion(bf16[1,288,3584]{2,1,0:T(8,128)(2,1)S(1)} %copy-done, bf16[2,288,3584]{2,1,0:T(8,128)(2,1)S(1)} %fusion), kind=kLoop, calls=%fused_computation.2 | loop fusion | flops 7225344 | bytes 8257536 | tf_op jit(solution)/shard_map/convert_element_type | solution.py:53
  184.3 2.0 %collective-permute-done.7 = bf16[2,128,288]{1,2,0:T(8,128)(2,1)S(1)} collective-permute-done((bf16[2,128,288]{1,2,0:T(8,128)(2,1)S(1)}, bf16[2,128,288]{1,2,0:T(8,128)(2,1)S(1)}, u32[]{:S(2)}, u32[]{:S(2)}) %collective-permute-start.7) | collective-permute-done | bytes 147488 | tf_op jit(solution)/shard_map/ppermute | solution.py:16
  186.3 0.7 maximum_bitcast_fusion
  (6 shorter events, 0.1 us)
Async XLA Ops:
  7.2 138.2 %all-gather.2.cloned.1.call-start = ((), (), s32[]{:S(2)}) async-start(), calls=%async_computation | async-start | bytes 3784704 | tf_op jit(solution)/shard_map/all_gather | solution.py:43
  10.7 8.9 %collective-permute-start = (bf16[2,51200]{1,0:T(2,128)(2,1)S(1)}, bf16[2,51200]{1,0:T(2,128)(2,1)S(1)}, u32[]{:S(2)}, u32[]{:S(2)}) collective-permute-start(bf16[2,51200]{1,0:T(2,128)(2,1)S(1)} %pad_maximum_fusion), channel_id=1, source_target_pairs={{0,32},{32,0},{64,96},{96,64},{128,160},{160,128},{192,224},{224,1... | collective-permute-start | bytes 614408 | tf_op jit(solution)/shard_map/ppermute | solution.py:16
  19.6 14.0 %collective-permute-start.1 = (bf16[2,51200]{1,0:T(2,128)(2,1)S(1)}, bf16[2,51200]{1,0:T(2,128)(2,1)S(1)}, u32[]{:S(2)}, u32[]{:S(2)}) collective-permute-start(bf16[2,51200]{1,0:T(2,128)(2,1)S(1)} %collective-permute-done), channel_id=1, source_target_pairs={{0,64},{64,0},{32,96},{96,32},{128,192},{192,128},{160,224},{224,1... | collective-permute-start | bytes 614408 | tf_op jit(solution)/shard_map/ppermute | solution.py:16
  33.6 7.8 %collective-permute-start.2 = (bf16[2,51200]{1,0:T(2,128)(2,1)S(1)}, bf16[2,51200]{1,0:T(2,128)(2,1)S(1)}, u32[]{:S(2)}, u32[]{:S(2)}) collective-permute-start(bf16[2,51200]{1,0:T(2,128)(2,1)S(1)} %collective-permute-done.1), channel_id=1, source_target_pairs={{0,128},{128,0},{32,160},{160,32},{64,192},{192,64},{96,224},{224,... | collective-permute-start | bytes 614408 | tf_op jit(solution)/shard_map/ppermute | solution.py:16
  41.4 9.1 %collective-permute-start.3 = (bf16[2,51200]{1,0:T(2,128)(2,1)S(1)}, bf16[2,51200]{1,0:T(2,128)(2,1)S(1)}, u32[]{:S(2)}, u32[]{:S(2)}) collective-permute-start(bf16[2,51200]{1,0:T(2,128)(2,1)S(1)} %collective-permute-done.2), channel_id=1, source_target_pairs={{0,256},{256,0},{32,288},{288,32},{64,320},{320,64},{96,352},{352,... | collective-permute-start | bytes 614408 | tf_op jit(solution)/shard_map/ppermute | solution.py:16
  149.4 7.9 %collective-permute-start.4 = (bf16[2,128,288]{1,2,0:T(8,128)(2,1)S(1)}, bf16[2,128,288]{1,2,0:T(8,128)(2,1)S(1)}, u32[]{:S(2)}, u32[]{:S(2)}) collective-permute-start(bf16[2,128,288]{1,2,0:T(8,128)(2,1)S(1)} %get-tuple-element.5), channel_id=1, source_target_pairs={{0,32},{32,0},{64,96},{96,64},{128,160},{160,128},{192,224},{224,1... | collective-permute-start | bytes 442376 | tf_op jit(solution)/shard_map/ppermute | solution.py:16
  157.3 11.2 %collective-permute-start.5 = (bf16[2,128,288]{1,2,0:T(8,128)(2,1)S(1)}, bf16[2,128,288]{1,2,0:T(8,128)(2,1)S(1)}, u32[]{:S(2)}, u32[]{:S(2)}) collective-permute-start(bf16[2,128,288]{1,2,0:T(8,128)(2,1)S(1)} %collective-permute-done.4), channel_id=1, source_target_pairs={{0,64},{64,0},{32,96},{96,32},{128,192},{192,128},{160,224},{224,1... | collective-permute-start | bytes 442376 | tf_op jit(solution)/shard_map/ppermute | solution.py:16
  168.5 9.0 %collective-permute-start.6 = (bf16[2,128,288]{1,2,0:T(8,128)(2,1)S(1)}, bf16[2,128,288]{1,2,0:T(8,128)(2,1)S(1)}, u32[]{:S(2)}, u32[]{:S(2)}) collective-permute-start(bf16[2,128,288]{1,2,0:T(8,128)(2,1)S(1)} %collective-permute-done.5), channel_id=1, source_target_pairs={{0,128},{128,0},{32,160},{160,32},{64,192},{192,64},{96,224},{224,... | collective-permute-start | bytes 442376 | tf_op jit(solution)/shard_map/ppermute | solution.py:16
  173.4 8.8 %copy-start = (bf16[1,288,3584]{2,1,0:T(8,128)(2,1)S(1)}, bf16[1,288,3584]{2,1,0:T(8,128)(2,1)}, u32[]{:S(2)}) copy-start(bf16[1,288,3584]{2,1,0:T(8,128)(2,1)} %param.6) | copy-start | bytes 6193156
  177.5 8.8 %collective-permute-start.7 = (bf16[2,128,288]{1,2,0:T(8,128)(2,1)S(1)}, bf16[2,128,288]{1,2,0:T(8,128)(2,1)S(1)}, u32[]{:S(2)}, u32[]{:S(2)}) collective-permute-start(bf16[2,128,288]{1,2,0:T(8,128)(2,1)S(1)} %collective-permute-done.6), channel_id=1, source_target_pairs={{0,256},{256,0},{32,288},{288,32},{64,320},{320,64},{96,352},{352,... | collective-permute-start | bytes 442376 | tf_op jit(solution)/shard_map/ppermute | solution.py:16
Sparse Core Ops, SparseCore 0:
  51.6 93.7 all-gather.1
where the time goes:
time: 194 us
  waiting for transfers between devices  131 us (68%)
  starting transfers between devices  32.5 us (17%)
  between operations  14.2 us (7%)
  matrix products  8.07 us (4%)
  other arithmetic  5.64 us (3%)
  local copies, waits for them, and re-layouts  2.22 us (1%)
    all_gather x1, waiting for transfers between devices, shards(): piece = lax.all_gather(both_masked, 'dp', axis=2, tiled=True)  93.9 us
    ppermute x8, waiting for transfers between devices, from_partner(): return lax.ppermute(block, axis, route)  37.4 us
    ppermute x8, starting transfers between devices, from_partner(): return lax.ppermute(block, axis, route)  32.5 us
    dot_general x1, matrix products, shards(): jnp.einsum('rmkh,rmkd->rhd', both_hidden, piece, preferred_element_type=j...  4.1 us
    dot_general x1, matrix products, shards(): jnp.einsum('rmkd,hd->rmkh', piece, own_weight, preferred_element_type=jnp...  3.97 us
  transfers between devices with their start and end apart: 9, of which 8 were waited for; matrix products, arithmetic and copies ran while one was open for 4% of the time, Pallas kernels for 0%

commit v1 on v0

--- a/solution.py
+++ b/solution.py
@@ -40,7 +40,8 @@
     mirror_masked, mirror_hidden = (mirror_masked, mirror_hidden)
     both_masked = jnp.stack([masked[0, 0], mirror_masked], axis=0)
     both_hidden = jnp.stack([hidden[0, 0], mirror_hidden], axis=0)
-    piece = lax.all_gather(both_masked, "dp", axis=2, tiled=True)
+    sent = jnp.stack([both_masked] * lax.axis_size("dp"))
+    piece = jnp.concatenate(lax.all_to_all(sent, "dp", 0, 0), axis=2)
     rows_out = jnp.einsum("rmkd,hd->rmkh", piece, own_weight, preferred_element_type=jnp.float32)
     grad_acc = rows_out
     weight_acc = jnp.einsum(

time: 194 us -> 278 us (1.43)
  the two profiles are of different devices: /device:TPU:4 before, /device:TPU:16 now
where the time goes in v1:
time: 278 us; the launch traced here: 277 us
  blocking collectives  181 us (65%)
  waiting for transfers between devices  42.6 us (15%)
  starting transfers between devices  26.9 us (10%)
  local copies, waits for them, and re-layouts  13.9 us (5%)
  matrix products  6.57 us (2%)
  other arithmetic  4.94 us (2%)
    all_to_all x1, blocking collectives, shards(): piece = jnp.concatenate(lax.all_to_all(sent, 'dp', 0, 0), axis=2)  181 us
    ppermute x8, waiting for transfers between devices, from_partner(): return lax.ppermute(block, axis, route)  42.6 us
    ppermute x8, starting transfers between devices, from_partner(): return lax.ppermute(block, axis, route)  26.9 us
    reshape x2, local copies, waits for them, and re-layouts, shards(): piece = jnp.concatenate(lax.all_to_all(sent, 'dp', 0, 0), axis=2)  9.95 us
  transfers between devices with their start and end apart: 8, of which 8 were waited for; matrix products, arithmetic and copies ran while one was open for 2% of the time, Pallas kernels for 0%

profile of v1, /device:TPU:16, one launch (start us, length us, event | category | flops | bytes accessed | tf_op | source)
XLA Modules:
  0.0 277.0 jit_solution(10693454347659125273)
XLA Ops:
  0.6 0.8 iota_compare_fusion
  1.4 1.0 broadcast_select_fusion
  2.5 1.0 slice_bitcast_fusion.1
  3.5 0.2 copy.8
  3.7 0.3 reshape_squeeze.7
  4.0 0.2 pad_maximum_fusion
  4.2 3.8 %collective-permute-start = (bf16[2,51200]{1,0:T(2,128)(2,1)S(1)}, bf16[2,51200]{1,0:T(2,128)(2,1)S(1)}, u32[]{:S(2)}, u32[]{:S(2)}) collective-permute-start(bf16[2,51200]{1,0:T(2,128)(2,1)S(1)} %pad_maximum_fusion), channel_id=1, source_target_pairs={{0,32},{32,0},{64,96},{96,64},{128,160},{160,128},{192,224},{224,1... | collective-permute-start | bytes 614408 | tf_op jit(solution)/shard_map/ppermute | solution.py:16
  8.0 5.1 %collective-permute-done = bf16[2,51200]{1,0:T(2,128)(2,1)S(1)} collective-permute-done((bf16[2,51200]{1,0:T(2,128)(2,1)S(1)}, bf16[2,51200]{1,0:T(2,128)(2,1)S(1)}, u32[]{:S(2)}, u32[]{:S(2)}) %collective-permute-start) | collective-permute-done | bytes 204832 | tf_op jit(solution)/shard_map/ppermute | solution.py:16
  13.1 5.2 %collective-permute-start.1 = (bf16[2,51200]{1,0:T(2,128)(2,1)S(1)}, bf16[2,51200]{1,0:T(2,128)(2,1)S(1)}, u32[]{:S(2)}, u32[]{:S(2)}) collective-permute-start(bf16[2,51200]{1,0:T(2,128)(2,1)S(1)} %collective-permute-done), channel_id=1, source_target_pairs={{0,64},{64,0},{32,96},{96,32},{128,192},{192,128},{160,224},{224,1... | collective-permute-start | bytes 614408 | tf_op jit(solution)/shard_map/ppermute | solution.py:16
  18.3 8.8 %collective-permute-done.1 = bf16[2,51200]{1,0:T(2,128)(2,1)S(1)} collective-permute-done((bf16[2,51200]{1,0:T(2,128)(2,1)S(1)}, bf16[2,51200]{1,0:T(2,128)(2,1)S(1)}, u32[]{:S(2)}, u32[]{:S(2)}) %collective-permute-start.1) | collective-permute-done | bytes 204832 | tf_op jit(solution)/shard_map/ppermute | solution.py:16
  27.0 3.2 %collective-permute-start.2 = (bf16[2,51200]{1,0:T(2,128)(2,1)S(1)}, bf16[2,51200]{1,0:T(2,128)(2,1)S(1)}, u32[]{:S(2)}, u32[]{:S(2)}) collective-permute-start(bf16[2,51200]{1,0:T(2,128)(2,1)S(1)} %collective-permute-done.1), channel_id=1, source_target_pairs={{0,128},{128,0},{32,160},{160,32},{64,192},{192,64},{96,224},{224,... | collective-permute-start | bytes 614408 | tf_op jit(solution)/shard_map/ppermute | solution.py:16
  30.2 4.7 %collective-permute-done.2 = bf16[2,51200]{1,0:T(2,128)(2,1)S(1)} collective-permute-done((bf16[2,51200]{1,0:T(2,128)(2,1)S(1)}, bf16[2,51200]{1,0:T(2,128)(2,1)S(1)}, u32[]{:S(2)}, u32[]{:S(2)}) %collective-permute-start.2) | collective-permute-done | bytes 204832 | tf_op jit(solution)/shard_map/ppermute | solution.py:16
  34.9 2.4 collective-permute-start.3
  37.3 6.8 %collective-permute-done.3 = bf16[2,51200]{1,0:T(2,128)(2,1)S(1)} collective-permute-done((bf16[2,51200]{1,0:T(2,128)(2,1)S(1)}, bf16[2,51200]{1,0:T(2,128)(2,1)S(1)}, u32[]{:S(2)}, u32[]{:S(2)}) %collective-permute-start.3) | collective-permute-done | bytes 204832 | tf_op jit(solution)/shard_map/ppermute | solution.py:16
  44.2 1.6 stack.11
  45.9 181.3 %all_to_all.5 = bf16[32,2,2,4,3584]{4,3,2,1,0:T(4,128)(2,1)S(1)} all-to-all(bf16[32,2,2,4,3584]{4,3,2,1,0:T(4,128)(2,1)S(1)} %stack.11), channel_id=1, replica_groups=mesh['pipe'=16,'dp'=32] {'dp'}, dimensions={0} | all-to-all | bytes 7340032 | tf_op jit(solution)/shard_map/all_to_all | solution.py:44
  227.2 3.1 %copy.9 = bf16[2,2,32,4,3584]{4,3,2,1,0:T(4,128)(2,1)} copy(bf16[2,2,32,4,3584]{4,3,1,0,2:T(4,128)(2,1)S(1)} %bitcast.35) | data formatting | bytes 7340032 | tf_op jit(solution)/shard_map/reshape | solution.py:44
  230.3 6.9 %reshape.22 = bf16[2,2,128,3584]{3,2,1,0:T(8,128)(2,1)} reshape(bf16[2,2,32,4,3584]{4,3,2,1,0:T(4,128)(2,1)} %copy.9) | data formatting | bytes 7340032 | tf_op jit(solution)/shard_map/reshape | solution.py:44
  237.2 3.3 %fusion.6 = bf16[2,2,128,288]{2,3,1,0:T(8,128)(2,1)S(1)} fusion(bf16[2,2,128,3584]{3,2,1,0:T(8,128)(2,1)} %reshape.22, bf16[1,288,3584]{2,1,0:T(8,128)(2,1)S(1)} %copy-done), kind=kOutput, calls=%fused_computation.6 | convolution fusion | flops 1057259520 | bytes 6029312 | tf_op jit(solution)/shard_map/rmkd,hd->rmkh/dot_general | solution.py:45
  240.5 1.9 collective-permute-start.4
  242.4 6.4 %collective-permute-done.4 = bf16[2,128,288]{1,2,0:T(8,128)(2,1)S(1)} collective-permute-done((bf16[2,128,288]{1,2,0:T(8,128)(2,1)S(1)}, bf16[2,128,288]{1,2,0:T(8,128)(2,1)S(1)}, u32[]{:S(2)}, u32[]{:S(2)}) %collective-permute-start.4) | collective-permute-done | bytes 147488 | tf_op jit(solution)/shard_map/ppermute | solution.py:16
  248.8 5.0 %collective-permute-start.5 = (bf16[2,128,288]{1,2,0:T(8,128)(2,1)S(1)}, bf16[2,128,288]{1,2,0:T(8,128)(2,1)S(1)}, u32[]{:S(2)}, u32[]{:S(2)}) collective-permute-start(bf16[2,128,288]{1,2,0:T(8,128)(2,1)S(1)} %collective-permute-done.4), channel_id=1, source_target_pairs={{0,64},{64,0},{32,96},{96,32},{128,192},{192,128},{160,224},{224,1... | collective-permute-start | bytes 442376 | tf_op jit(solution)/shard_map/ppermute | solution.py:16
  253.9 0.3 stack_reshape.7
  254.2 0.2 copy.10
  254.4 5.7 %collective-permute-done.5 = bf16[2,128,288]{1,2,0:T(8,128)(2,1)S(1)} collective-permute-done((bf16[2,128,288]{1,2,0:T(8,128)(2,1)S(1)}, bf16[2,128,288]{1,2,0:T(8,128)(2,1)S(1)}, u32[]{:S(2)}, u32[]{:S(2)}) %collective-permute-start.5) | collective-permute-done | bytes 147488 | tf_op jit(solution)/shard_map/ppermute | solution.py:16
  260.1 3.2 %collective-permute-start.6 = (bf16[2,128,288]{1,2,0:T(8,128)(2,1)S(1)}, bf16[2,128,288]{1,2,0:T(8,128)(2,1)S(1)}, u32[]{:S(2)}, u32[]{:S(2)}) collective-permute-start(bf16[2,128,288]{1,2,0:T(8,128)(2,1)S(1)} %collective-permute-done.5), channel_id=1, source_target_pairs={{0,128},{128,0},{32,160},{160,32},{64,192},{192,64},{96,224},{224,... | collective-permute-start | bytes 442376 | tf_op jit(solution)/shard_map/ppermute | solution.py:16
  263.3 3.3 %fusion = bf16[2,288,3584]{2,1,0:T(8,128)(2,1)S(1)} fusion(bf16[2,2,128,3584]{3,2,1,0:T(8,128)(2,1)} %reshape.22, bf16[1,2,128,288]{2,3,1,0:T(8,128)(2,1)S(1)} %copy.10, bf16[1,2,128,288]{2,3,1,0:T(8,128)(2,1)S(1)} %get-tuple-element.2), kind=kOutput, calls=%fused_computation.1 | convolution fusion | flops 1061240832 | bytes 8093696 | tf_op jit(solution)/shard_map/rmkh,rmkd->rhd/dot_general | solution.py:47
  266.6 1.2 collective-permute-done.6
  267.7 2.2 collective-permute-start.7
  270.0 2.2 subtract_convert_fusion
  272.2 4.1 %collective-permute-done.7 = bf16[2,128,288]{1,2,0:T(8,128)(2,1)S(1)} collective-permute-done((bf16[2,128,288]{1,2,0:T(8,128)(2,1)S(1)}, bf16[2,128,288]{1,2,0:T(8,128)(2,1)S(1)}, u32[]{:S(2)}, u32[]{:S(2)}) %collective-permute-start.7) | collective-permute-done | bytes 147488 | tf_op jit(solution)/shard_map/ppermute | solution.py:16
  276.3 0.7 maximum_bitcast_fusion
  (9 shorter events, 0.4 us)
Async XLA Ops:
  4.2 8.9 %collective-permute-start = (bf16[2,51200]{1,0:T(2,128)(2,1)S(1)}, bf16[2,51200]{1,0:T(2,128)(2,1)S(1)}, u32[]{:S(2)}, u32[]{:S(2)}) collective-permute-start(bf16[2,51200]{1,0:T(2,128)(2,1)S(1)} %pad_maximum_fusion), channel_id=1, source_target_pairs={{0,32},{32,0},{64,96},{96,64},{128,160},{160,128},{192,224},{224,1... | collective-permute-start | bytes 614408 | tf_op jit(solution)/shard_map/ppermute | solution.py:16
  13.1 14.0 %collective-permute-start.1 = (bf16[2,51200]{1,0:T(2,128)(2,1)S(1)}, bf16[2,51200]{1,0:T(2,128)(2,1)S(1)}, u32[]{:S(2)}, u32[]{:S(2)}) collective-permute-start(bf16[2,51200]{1,0:T(2,128)(2,1)S(1)} %collective-permute-done), channel_id=1, source_target_pairs={{0,64},{64,0},{32,96},{96,32},{128,192},{192,128},{160,224},{224,1... | collective-permute-start | bytes 614408 | tf_op jit(solution)/shard_map/ppermute | solution.py:16
  27.0 7.8 %collective-permute-start.2 = (bf16[2,51200]{1,0:T(2,128)(2,1)S(1)}, bf16[2,51200]{1,0:T(2,128)(2,1)S(1)}, u32[]{:S(2)}, u32[]{:S(2)}) collective-permute-start(bf16[2,51200]{1,0:T(2,128)(2,1)S(1)} %collective-permute-done.1), channel_id=1, source_target_pairs={{0,128},{128,0},{32,160},{160,32},{64,192},{192,64},{96,224},{224,... | collective-permute-start | bytes 614408 | tf_op jit(solution)/shard_map/ppermute | solution.py:16
  34.9 9.1 %collective-permute-start.3 = (bf16[2,51200]{1,0:T(2,128)(2,1)S(1)}, bf16[2,51200]{1,0:T(2,128)(2,1)S(1)}, u32[]{:S(2)}, u32[]{:S(2)}) collective-permute-start(bf16[2,51200]{1,0:T(2,128)(2,1)S(1)} %collective-permute-done.2), channel_id=1, source_target_pairs={{0,256},{256,0},{32,288},{288,32},{64,320},{320,64},{96,352},{352,... | collective-permute-start | bytes 614408 | tf_op jit(solution)/shard_map/ppermute | solution.py:16
  230.3 6.9 %copy-start = (bf16[1,288,3584]{2,1,0:T(8,128)(2,1)S(1)}, bf16[1,288,3584]{2,1,0:T(8,128)(2,1)}, u32[]{:S(2)}) copy-start(bf16[1,288,3584]{2,1,0:T(8,128)(2,1)} %param.6) | copy-start | bytes 6193156
  240.5 8.3 %collective-permute-start.4 = (bf16[2,128,288]{1,2,0:T(8,128)(2,1)S(1)}, bf16[2,128,288]{1,2,0:T(8,128)(2,1)S(1)}, u32[]{:S(2)}, u32[]{:S(2)}) collective-permute-start(bf16[2,128,288]{1,2,0:T(8,128)(2,1)S(1)} %get-tuple-element.5), channel_id=1, source_target_pairs={{0,32},{32,0},{64,96},{96,64},{128,160},{160,128},{192,224},{224,1... | collective-permute-start | bytes 442376 | tf_op jit(solution)/shard_map/ppermute | solution.py:16
  248.8 11.3 %collective-permute-start.5 = (bf16[2,128,288]{1,2,0:T(8,128)(2,1)S(1)}, bf16[2,128,288]{1,2,0:T(8,128)(2,1)S(1)}, u32[]{:S(2)}, u32[]{:S(2)}) collective-permute-start(bf16[2,128,288]{1,2,0:T(8,128)(2,1)S(1)} %collective-permute-done.4), channel_id=1, source_target_pairs={{0,64},{64,0},{32,96},{96,32},{128,192},{192,128},{160,224},{224,1... | collective-permute-start | bytes 442376 | tf_op jit(solution)/shard_map/ppermute | solution.py:16
  260.1 7.7 %collective-permute-start.6 = (bf16[2,128,288]{1,2,0:T(8,128)(2,1)S(1)}, bf16[2,128,288]{1,2,0:T(8,128)(2,1)S(1)}, u32[]{:S(2)}, u32[]{:S(2)}) collective-permute-start(bf16[2,128,288]{1,2,0:T(8,128)(2,1)S(1)} %collective-permute-done.5), channel_id=1, source_target_pairs={{0,128},{128,0},{32,160},{160,32},{64,192},{192,64},{96,224},{224,... | collective-permute-start | bytes 442376 | tf_op jit(solution)/shard_map/ppermute | solution.py:16
  267.7 8.5 %collective-permute-start.7 = (bf16[2,128,288]{1,2,0:T(8,128)(2,1)S(1)}, bf16[2,128,288]{1,2,0:T(8,128)(2,1)S(1)}, u32[]{:S(2)}, u32[]{:S(2)}) collective-permute-start(bf16[2,128,288]{1,2,0:T(8,128)(2,1)S(1)} %collective-permute-done.6), channel_id=1, source_target_pairs={{0,256},{256,0},{32,288},{288,32},{64,320},{320,64},{96,352},{352,... | collective-permute-start | bytes 442376 | tf_op jit(solution)/shard_map/ppermute | solution.py:16
